TPU v7x, 256 devices: a whole 4x4x8 slice. The times are simulated.
256 devices in a mesh: walk: 16 (over z, x_hi), blk: 16 (over x_lo, y, core).
Axes of the slice: x: 4 (x_hi: 2, x_lo: 2; x = x_hi * 2 + x_lo), y: 4, z: 8, core: 2. Of those that a mesh axis runs over, the one named last changes fastest.
Arguments:
- vertex_times: int32 [16, 1024], P('blk'), may hold values from 0 to 4095
- vertex_sites: int32 [16, 1024], P('blk'), may hold values from 0 to 15
- vertex_matrix: bfloat16 [16, 1024, 1024], P('blk', 'walk'), may hold values from -0.1875 to 0.1875
- bare_green: float32 [2, 1024], replicated, may hold values from -3 to 3
- transfer_momentum: int32 [16], replicated, may hold values from 0 to 15, each once
- transfers: int32 [32], replicated, may hold values from 0 to 31, each once
Outputs:
- g4: float32 [2, 32, 1024, 1024], P(None, 'blk', 'walk')
Inputs may be any that keep to these rules, and one draw needn't show every extreme that they name: `transfer_momentum`: each of 0 to 15 appears exactly once. `transfers`: each of 0 to 31 appears exactly once.
All inputs are finite; a program needn't handle non-finite values.
Results may differ from a plain program's by a relative error of at most 0.0071.
Values may be sent and summed in bfloat16 or wider, within the bound.
A program may use at most 64 MiB of HBM per device.

v0:
```python
import math

import jax
import jax.numpy as jnp
from jax import lax
from jax.sharding import PartitionSpec as P

NM = 16
NF = 64
NV = 1024
NT = 4096
QB = 2


side_length = 4


def fourier_table(times, sites):
    points = jnp.arange(NM * NF, dtype=jnp.int32)
    momentum = points // NF
    frequency = points % NF
    momentum_x = momentum // side_length
    momentum_y = momentum % side_length
    site_x = sites // side_length
    site_y = sites % side_length
    odd_part = 4 * (2 * frequency + 1 - NF)
    phase = odd_part[:, None] * times[None, :] - 2 * NT * (
        momentum_x[:, None] * site_x[None, :] + momentum_y[:, None] * site_y[None, :]
    )
    phase = jnp.mod(phase, 8 * NT)
    angle = phase.astype(jnp.float32) * (2.0 * math.pi / (8 * NT))
    return (jnp.cos(angle).astype(jnp.bfloat16), jnp.sin(angle).astype(jnp.bfloat16))


def assemble(spread_re, spread_im, row_re, row_im, col_re, col_im, rows, cols):
    scale = NV ** (-0.5)
    part_re = (spread_re * col_re[None, :] - spread_im * col_im[None, :]) * scale
    part_im = (spread_re * col_im[None, :] + spread_im * col_re[None, :]) * scale
    diagonal = (rows[:, None] == cols[None, :]).astype(jnp.float32)
    green_re = row_re[:, None] * (part_re + diagonal) - row_im[:, None] * part_im
    green_im = row_re[:, None] * part_im + row_im[:, None] * (part_re + diagonal)
    return (green_re.astype(jnp.bfloat16), green_im.astype(jnp.bfloat16))


def send_layout(panels, shift):
    count = panels.shape[0]
    row_count = panels.shape[2]
    grid = panels.reshape(count, 2, row_count, NM, NF)
    grid = jnp.take(grid, shift, axis=3)
    grid = jnp.transpose(grid, (0, 1, 3, 2, 4))
    return grid.reshape(count, 2, 1, NM, row_count * NF)


def receive_layout(incoming, shift):
    count, _, groups, moments, flat = incoming.shape
    row_count = flat // NF
    grid = incoming.reshape(count, 2, groups, moments, row_count, NF)
    grid = jnp.transpose(grid, (0, 1, 3, 5, 2, 4))
    grid = jnp.take(grid, shift, axis=4)
    return grid.reshape(count, 2, moments * NF, NM * NF)


def accumulate(total, direct, turned, offsets):
    moments = turned.shape[1] // NF
    grid = turned.reshape(2, moments, NF, NM, NF)
    near = direct.astype(jnp.float32)
    spots = jnp.arange(NF, dtype=jnp.int32)
    for position in range(offsets.shape[0]):
        offset = offsets[position]
        rolled = jnp.roll(grid, -offset, axis=2)
        rolled = jnp.roll(rolled, -offset, axis=4)
        valid = (spots + offset >= 0) & (spots + offset < NF)
        keep = valid[:, None, None] & valid[None, None, :]
        masked = jnp.where(keep[None, None], rolled, jnp.zeros((), rolled.dtype))
        shifted = masked.reshape(2, moments * NF, NM * NF).astype(jnp.float32)
        part_re = near[0] * shifted[0] - near[1] * shifted[1]
        part_im = near[0] * shifted[1] + near[1] * shifted[0]
        total = total.at[:, position].add(jnp.stack([part_re, part_im]))
    return total


def walker_sum(total, direct_panels, turned_panels, offsets):

    def step(carry, pair):
        return (accumulate(carry, pair[0], pair[1], offsets), None)

    result, _ = lax.scan(step, total, (direct_panels, turned_panels))
    return result


def shards(vertex_times, vertex_sites, vertex_matrix, bare_green, transfer_momentum, transfers):
    walk_count = lax.axis_size("walk")
    walk_index = lax.axis_index("walk")
    blk_index = lax.axis_index("blk")
    points = NM * NF
    row_count = points // walk_count
    four_re, four_im = fourier_table(vertex_times[0], vertex_sites[0])
    row_start = walk_index * row_count
    rows_re = lax.dynamic_slice_in_dim(four_re, row_start, row_count, 0)
    rows_im = lax.dynamic_slice_in_dim(four_im, row_start, row_count, 0)
    piece = lax.all_gather(vertex_matrix[0], "walk", axis=0, tiled=True)
    inner_re = jnp.dot(rows_re, piece, preferred_element_type=jnp.float32)
    inner_im = jnp.dot(rows_im, piece, preferred_element_type=jnp.float32)
    inner_re = inner_re.astype(jnp.bfloat16)
    inner_im = inner_im.astype(jnp.bfloat16)
    contract = (((1,), (1,)), ((), ()))

    def product(left, right):
        return lax.dot_general(left, right, contract, preferred_element_type=jnp.float32)

    spread_re = product(inner_re, four_re) + product(inner_im, four_im)
    spread_im = product(inner_im, four_re) - product(inner_re, four_im)
    rows = row_start + jnp.arange(row_count, dtype=jnp.int32)
    cols = jnp.arange(points, dtype=jnp.int32)
    row_re = lax.dynamic_slice_in_dim(bare_green[0], row_start, row_count)
    row_im = lax.dynamic_slice_in_dim(bare_green[1], row_start, row_count)
    green_re, green_im = assemble(
        spread_re, spread_im, row_re, row_im, bare_green[0], bare_green[1], rows, cols
    )
    direct = jnp.stack([green_re, green_im])
    window_size = transfers.shape[0]
    offsets = lax.dynamic_slice_in_dim(transfers, blk_index * QB, QB) - window_size // 2
    slab = jnp.zeros((2, QB, row_count, points), jnp.float32)
    outgoing = send_layout(direct[None], transfer_momentum)
    incoming = lax.all_to_all(outgoing, "walk", split_axis=3, concat_axis=2, tiled=True)
    turned = receive_layout(incoming, transfer_momentum)
    return walker_sum(
        slab,
        lax.all_gather(direct[None], "blk", axis=0, tiled=True),
        lax.all_gather(turned, "blk", axis=0, tiled=True),
        offsets,
    )


def solution(mesh):
    return jax.shard_map(
        shards,
        mesh=mesh,
        in_specs=(P("blk", None), P("blk", None), P("blk", "walk", None), P(), P(), P()),
        out_specs=P(None, "blk", "walk", None),
        check_vma=False,
    )
```

profile of v0, /device:TPU:1, one launch (start us, length us, event | category | flops | bytes accessed | tf_op | source)
XLA Modules:
  0.0 327.7 jit_solution(9244534965251903392)
XLA Ops:
  8.9 20.1 %cosine_convert_fusion = (bf16[1024,1024]{1,0:T(8,128)(2,1)S(1)}, bf16[1024,1024]{1,0:T(8,128)(2,1)}) fusion(s32[1024]{0:T(1024)S(1)} %bitcast.120, s32[1024]{0:T(1024)S(1)} %get-tuple-element.158, s32[1024]{0:T(1024)S(1)} %bitcast.117, s32[1024]{0:T(1024)S(1)} %get-tuple-element.159, s32[1024]{0:T(1024)} %bitcast.125, s32[1024]{0:T(1024)S(1)} %fusion.25), kind=kLoop, calls=%fused_computation.38 | loop fusion | flops 22020096 | bytes 4218880 | tf_op jit(solution)/shard_map/convert_element_type | solution.py:32
  29.1 66.4 %all-gather.8.cloned.1.call-done = bf16[1,1024,1024]{2,1,0:T(8,128)(2,1)} async-done(((bf16[1,64,1024]{2,1,0:T(8,128)(2,1)}), bf16[1,1024,1024]{2,1,0:T(8,128)(2,1)}) %all-gather.8.cloned.1.call-update) | async-done | bytes 2097168 | tf_op jit(solution)/shard_map/all_gather | solution.py:101
  95.4 2.2 fusion.14
  98.5 1.4 fusion.17
  100.6 16.5 %convolution_add_fusion = f32[64,1024]{1,0:T(8,128)S(1)} fusion(f32[64,1024]{1,0:T(8,128)S(1)} %fusion.47, bf16[64,1024]{1,0:T(8,128)(2,1)S(1)} %fusion.17, s32[1024]{0:T(1024)S(1)} %bitcast.121, s32[1024]{0:T(1024)S(1)} %get-tuple-element.158, s32[1024]{0:T(1024)S(1)} %bitcast.118, s32[1024]{0:T(1024)S(1)} %get-tuple-element.159, s32[1024]{0:T(1024)S(1)} %bitcast.126, ...), kind=kOutput, calls=%fused_computation.44 | convolution fusion | flops 155254784 | bytes 679936 | tf_op jit(solution)/shard_map/dot_general | solution.py:109
  117.1 16.8 %subtract_convert_fusion = (bf16[64,1024]{1,0:T(8,128)(2,1)S(1)}, bf16[64,1024]{1,0:T(8,128)(2,1)S(1)}) fusion(f32[64]{0:T(128)S(1)} %get-tuple-element.156, f32[64]{0:T(128)S(1)} %get-tuple-element.129, f32[1024]{0:T(1024)S(1)} %bitcast.123, f32[64,1024]{1,0:T(8,128)S(1)} %convolution_add_fusion, f32[1024]{0:T(1024)S(1)} %bitcast.124, ...), kind=kOutput, calls=%fused_computation.52 | convolution fusion | flops 156434432 | bytes 951552 | tf_op jit(solution)/shard_map/dot_general | solution.py:109
  136.3 1.1 reshape.348
  137.4 4.0 %all-to-all-start = ((bf16[1,2,1,16,4096]{4,1,2,0,3:T(2,128)(2,1)}), bf16[1,2,1,16,4096]{4,1,2,0,3:T(2,128)(2,1)S(1)}, u32[]{:S(2)}, u32[]{:S(2)}) async-start(bf16[1,2,1,16,4096]{4,1,2,0,3:T(2,128)(2,1)} %bitcast.28), calls=%async_computation | async-start | bytes 524288 | tf_op jit(solution)/shard_map/all_to_all | solution.py:125
  141.7 11.0 %all-to-all-done = bf16[1,2,1,16,4096]{4,1,2,0,3:T(2,128)(2,1)S(1)} async-done(((bf16[1,2,1,16,4096]{4,1,2,0,3:T(2,128)(2,1)}), bf16[1,2,1,16,4096]{4,1,2,0,3:T(2,128)(2,1)S(1)}, u32[]{:S(2)}, u32[]{:S(2)}) %all-to-all-start) | async-done | bytes 262176 | tf_op jit(solution)/shard_map/all_to_all | solution.py:125
  157.5 18.7 %all-gather.10.cloned.1.call-done = bf16[32,64,1024]{2,1,0:T(8,128)(2,1)} async-done(((bf16[2,64,1024]{2,1,0:T(8,128)(2,1)}), bf16[32,64,1024]{2,1,0:T(8,128)(2,1)}) %all-gather.10.cloned.1.call-update) | async-done | bytes 4194320 | tf_op jit(solution)/shard_map/all_gather | solution.py:129
  176.1 42.0 %all-gather.6.cloned.1.call-done = bf16[16,2,64,1024]{3,2,1,0:T(8,128)(2,1)} async-done(((bf16[1,2,64,1024]{3,2,1,0:T(8,128)(2,1)}), bf16[16,2,64,1024]{3,2,1,0:T(8,128)(2,1)}) %all-gather.6.cloned.1.call-update) | async-done | bytes 4194320 | tf_op jit(solution)/shard_map/all_gather | solution.py:130
  218.2 101.8 %while.14 = (s32[]{:T(128)}, f32[2,2,64,1024]{3,2,1,0:T(8,128)S(1)}, bf16[16,2,64,1024]{3,2,1,0:T(8,128)(2,1)}, s32[2]{0:T(128)S(1)}, bf16[16,2,64,1024]{3,2,1,0...) while((s32[]{:T(128)}, ...), condition=%wide.region_1.4_spmd, body=%wide.region_0.3_spmd.sunk | while | flops 3023392 | bytes 18367192 | solution.py:87
  218.3 1.1 dynamic-slice_convert_fusion.2
  220.6 1.2 compare_and_fusion.4
  224.6 1.1 dynamic-slice_convert_fusion.2
  227.0 1.2 compare_and_fusion.4
  231.0 1.1 dynamic-slice_convert_fusion.2
  233.3 1.2 compare_and_fusion.4
  239.7 1.2 compare_and_fusion.4
  246.1 1.2 compare_and_fusion.4
  252.4 1.2 compare_and_fusion.4
  258.8 1.2 compare_and_fusion.4
  265.2 1.2 compare_and_fusion.4
  271.5 1.2 compare_and_fusion.4
  275.5 1.1 dynamic-slice_convert_fusion.2
  277.9 1.2 compare_and_fusion.4
  284.2 1.2 compare_and_fusion.4
  290.6 1.2 compare_and_fusion.4
  297.0 1.2 compare_and_fusion.4
  303.3 1.2 compare_and_fusion.4
  309.7 1.2 compare_and_fusion.4
  316.1 1.2 compare_and_fusion.4
  (363 shorter events, 86.5 us)
Async XLA Ops:
  6.5 88.9 %all-gather.8.cloned.1.call-start = ((), (), s32[]{:S(2)}) async-start(), calls=%async_computation.2 | async-start | bytes 2228224 | tf_op jit(solution)/shard_map/all_gather | solution.py:101
  7.3 168.9 %all-gather.10.cloned.1.call-start = ((), (), s32[]{:S(2)}) async-start(), calls=%async_computation.3 | async-start | bytes 4456448 | tf_op jit(solution)/shard_map/all_gather | solution.py:129
  95.4 3.0 copy-start.1
  97.7 2.9 copy-start.2
  117.1 17.6 %copy-start.3 = (s32[16]{0:T(128)S(1)}, s32[16]{0:T(128)}, u32[]{:S(2)}) copy-start(s32[16]{0:T(128)} %param.20) | copy-start | bytes 196
  136.2 19.3 %copy-start.4 = (s32[32]{0:T(128)S(1)}, s32[32]{0:T(128)}, u32[]{:S(2)}) copy-start(s32[32]{0:T(128)} %param.21) | copy-start | bytes 388
  137.4 15.2 %all-to-all-start = ((bf16[1,2,1,16,4096]{4,1,2,0,3:T(2,128)(2,1)}), bf16[1,2,1,16,4096]{4,1,2,0,3:T(2,128)(2,1)S(1)}, u32[]{:S(2)}, u32[]{:S(2)}) async-start(bf16[1,2,1,16,4096]{4,1,2,0,3:T(2,128)(2,1)} %bitcast.28), calls=%async_computation | async-start | bytes 524288 | tf_op jit(solution)/shard_map/all_to_all | solution.py:125
  141.5 76.6 %all-gather.6.cloned.1.call-start = ((), (), s32[]{:S(2)}) async-start(), calls=%async_computation.1 | async-start | bytes 4456448 | tf_op jit(solution)/shard_map/all_gather | solution.py:130
  320.0 1.0 copy-start
Sparse Core Ops, SparseCore 0:
  9.9 85.4 all-gather.7
  134.8 41.3 all-gather.9
  178.0 40.0 all-gather.5
where the time goes:
time: 331 us; the launch traced here: 328 us
  waiting for transfers between devices  139 us (42%)
  other arithmetic  87.8 us (27%)
  local copies, waits for them, and re-layouts  41.1 us (12%)
  matrix products  38.4 us (12%)
  between operations  14.8 us (4%)
  starting transfers between devices  4.11 us (1%)
    all_gather x1, waiting for transfers between devices, shards(): piece = lax.all_gather(vertex_matrix[0], 'walk', axis=0, tiled=True)  66.4 us
    all_gather x1, waiting for transfers between devices, shards(): lax.all_gather(turned, 'blk', axis=0, tiled=True)  42 us
    dot_general x4, matrix products, product(): lax.dot_general(left, right, contract, preferred_element_type=jnp.float32)  34.8 us
    convert_element_type x1, other arithmetic, fourier_table(): jnp.cos(angle).astype(jnp.bfloat16)  20.1 us
    convert_element_type x32, other arithmetic, accumulate(): shifted = masked.reshape(2, moments * NF, NM * NF).astype(jnp.float32)  19.8 us
    and x16, other arithmetic, accumulate(): valid = (spots + offset >= 0) & (spots + offset < NF)  19.1 us
    all_gather x1, waiting for transfers between devices, shards(): lax.all_gather(direct[None], 'blk', axis=0, tiled=True)  18.7 us
    convert_element_type x16, other arithmetic, accumulate(): near = direct.astype(jnp.float32)  17.6 us
  transfers between devices with their start and end apart: 4, of which 4 were waited for; matrix products, arithmetic and copies ran while one was open for 9% of the time, Pallas kernels for 0%

commit v1 on v0

v1 whole, which is shorter than its diff:
```python
import math

import jax
import jax.numpy as jnp
from jax import lax
from jax.experimental import pallas as pl
from jax.experimental.pallas import tpu as pltpu
from jax.sharding import PartitionSpec as P

NM = 16
NF = 64
NV = 1024
NT = 4096
NQ = 32
SIDE = 4
ND = 16
PACK = 2 * NF
TURN = 8 * NT
QUARTER = TURN // 4
MESH = pl.DeviceIdType.MESH
F32 = jnp.float32
BF16 = jnp.bfloat16


def sincos(phase):
    quadrant = (phase + QUARTER // 2) >> 13
    angle = (phase - (quadrant << 13)).astype(F32) * (2.0 * math.pi / TURN)
    square = angle * angle
    sine = angle * (
        1.0 + square * (-1.0 / 6 + square * (1.0 / 120 + square * (-1.0 / 5040 + square * (1.0 / 362880))))
    )
    cosine = 1.0 + square * (
        -0.5 + square * (1.0 / 24 + square * (-1.0 / 720 + square * (1.0 / 40320 - square * (1.0 / 3628800))))
    )
    odd = (quadrant & 1) == 1
    sign = (1 - (quadrant & 2)).astype(F32)
    return jnp.where(odd, -sine, cosine) * sign, jnp.where(odd, cosine, sine) * sign


def swap(value):
    return pltpu.roll(value, NF, 1)


def kernel(
    times,
    sites,
    matrix,
    bare,
    shift,
    transfers,
    out,
    base,
    table,
    outer_re,
    outer_im,
    inverse,
    send_a,
    recv_a,
    green,
    send_t,
    recv_d,
    recv_t,
    direct_re,
    direct_im,
    turned_re,
    turned_im,
    send_o,
    recv_o,
    sem_sa,
    sem_ra,
    sem_sd,
    sem_rd,
    sem_st,
    sem_rt,
    sem_so,
    sem_ro,
):
    w = lax.axis_index("walk")
    b = lax.axis_index("blk")
    source = lax.rem(b - w + ND, ND)
    twice = lax.rem(2 * w, ND)
    alone = twice == b

    barrier = pltpu.get_barrier_semaphore()

    def greet(i, carry):
        pl.semaphore_signal(barrier, inc=1, device_id=(lax.rem(w + i, ND), b), device_id_type=MESH)
        pl.semaphore_signal(barrier, inc=1, device_id=(w, lax.rem(b + i, ND)), device_id_type=MESH)
        return carry

    lax.fori_loop(1, ND, greet, 0)

    def greet_source(i, carry):
        @pl.when(jnp.logical_not(jnp.logical_and(alone, i == b)))
        def _():
            pl.semaphore_signal(barrier, inc=1, device_id=(source, i), device_id_type=MESH)

        return carry

    lax.fori_loop(0, ND, greet_source, 0)

    def base_rows(i, carry):
        first = pl.multiple_of(i * 16, 16)
        f = lax.broadcasted_iota(jnp.int32, (16, NV), 0) + first
        phase = (4 * (2 * f + 1 - NF) * times[...]) & (TURN - 1)
        cosine, sine = sincos(phase)
        base[0, pl.ds(first, 16), :] = cosine.astype(BF16)
        base[1, pl.ds(first, 16), :] = sine.astype(BF16)
        return carry

    lax.fori_loop(0, NF // 16, base_rows, 0)

    def rotate(m, carry):
        turn = ((m // SIDE) * (sites[...] >> 2) + (m % SIDE) * (sites[...] & 3)) & 3
        sign = (1 - (turn & 2)).astype(F32)
        odd = (turn & 1).astype(F32)
        along = jnp.broadcast_to((1.0 - odd) * sign, (NF, NV)).astype(BF16)
        across = jnp.broadcast_to(odd * sign, (NF, NV)).astype(BF16)
        cosine = base[0]
        sine = base[1]
        table[m, 0:NF, :] = cosine * along + sine * across
        table[m, NF:PACK, :] = sine * along - cosine * across
        return carry

    lax.fori_loop(0, NM, rotate, 0)

    def project(i, carry):
        block = lax.dot_general(
            matrix[0], table[shift[i]], (((1,), (1,)), ((), ())), preferred_element_type=F32
        )
        send_a[i] = block.astype(BF16)
        return carry

    lax.fori_loop(0, ND, project, 0)

    pl.semaphore_wait(barrier, 3 * ND - 2 - alone.astype(jnp.int32))

    def copy_a(peer):
        return pltpu.make_async_remote_copy(
            src_ref=send_a.at[peer],
            dst_ref=recv_a.at[pl.ds(pl.multiple_of(w * NF, NF), NF)],
            send_sem=sem_sa.at[peer],
            recv_sem=sem_ra.at[w],
            device_id=(peer, b),
            device_id_type=MESH,
        )

    def start_a(i, carry):
        copy_a(lax.rem(w + i, ND)).start()
        return carry

    lax.fori_loop(1, ND, start_a, 0)
    recv_a[pl.ds(pl.multiple_of(w * NF, NF), NF), :] = send_a[w]

    for part, target in ((0, outer_re), (1, outer_im)):
        for tile in range(NV // 128):
            row = jnp.broadcast_to(bare[part : part + 1, tile * 128 : tile * 128 + 128], (128, 128))
            target[tile * 128 : tile * 128 + 128, :] = row.T

    for m in range(NM):
        position = jnp.int32(0)
        for i in range(1, NM):
            position = jnp.where(shift[i] == m, i, position)
        inverse[m] = position

    for target in (turned_re, turned_im):
        for pair in range(NM // 2):
            target[pair, 0:16, :] = jnp.zeros((16, 128), F32)
            target[pair, 80:96, :] = jnp.zeros((16, 128), F32)

    left = lax.broadcasted_iota(jnp.int32, (NF, PACK), 1) < NF
    row_of = lax.broadcasted_iota(jnp.int32, (NF, PACK), 0)
    lane_of = lax.broadcasted_iota(jnp.int32, (NF, PACK), 1) & (NF - 1)
    minus_right = jnp.where(left, 1.0, -1.0)
    minus_left = -minus_right
    mine = shift[w]
    col_re = bare[0:1, 0:NF]
    col_im = bare[1:2, 0:NF]
    for m in range(1, NM):
        col_re = jnp.where(mine == m, bare[0:1, m * NF : m * NF + NF], col_re)
        col_im = jnp.where(mine == m, bare[1:2, m * NF : m * NF + NF], col_im)
    scale = NV ** (-0.5)
    col_re = jnp.concatenate([col_re, col_re], axis=1) * scale
    col_im = jnp.concatenate([-col_im, col_im], axis=1) * scale

    def arrive_a(i, carry):
        peer = lax.rem(w + i, ND)
        pltpu.make_async_remote_copy(
            src_ref=send_a.at[peer],
            dst_ref=recv_a.at[pl.ds(pl.multiple_of(peer * NF, NF), NF)],
            send_sem=sem_sa.at[peer],
            recv_sem=sem_ra.at[peer],
            device_id=(peer, b),
            device_id_type=MESH,
        ).wait()
        return carry

    lax.fori_loop(1, ND, arrive_a, 0)

    def copy_d(m):
        return pltpu.make_async_remote_copy(
            src_ref=green.at[m],
            dst_ref=recv_d.at[b],
            send_sem=sem_sd.at[m],
            recv_sem=sem_rd.at[b],
            device_id=(m, lax.rem(w + m, ND)),
            device_id_type=MESH,
        )

    def own_d(m):
        return pltpu.make_async_copy(green.at[m], recv_d.at[b], sem_rd.at[b])

    def is_own(m):
        return jnp.logical_and(alone, m == w)

    def assemble(group, carry):
        first = group * 4
        rows = table[pl.ds(first, 4)].reshape(4 * PACK, NV)
        raw = jnp.dot(rows, recv_a[...], preferred_element_type=F32)
        for k in range(4):
            m = first + k
            spread = raw[k * PACK : k * PACK + NF] * minus_right + swap(raw[k * PACK + NF : (k + 1) * PACK])
            part = spread * col_re + swap(spread) * col_im
            part = part + jnp.where(jnp.logical_and(left, row_of == lane_of), (mine == m).astype(F32), 0.0)
            start = pl.multiple_of(m * NF, NF)
            value = outer_re[pl.ds(start, NF), :] * part + outer_im[pl.ds(start, NF), :] * minus_left * swap(part)
            green[m] = value.astype(BF16)
        for k in range(4):
            m = first + k

            @pl.when(jnp.logical_not(is_own(m)))
            def _():
                copy_d(m).start()

            @pl.when(is_own(m))
            def _():
                own_d(m).start()

        return carry

    lax.fori_loop(0, NM // 4, assemble, 0)

    def copy_t(peer):
        return pltpu.make_async_remote_copy(
            src_ref=send_t.at[peer],
            dst_ref=recv_t.at[b],
            send_sem=sem_st.at[peer],
            recv_sem=sem_rt.at[b],
            device_id=(w, peer),
            device_id_type=MESH,
        )

    def start_t(i, carry):
        peer = lax.rem(b + i, ND)
        send_t[peer] = green[shift[shift[lax.rem(peer - w + ND, ND)]]]
        copy_t(peer).start()
        return carry

    lax.fori_loop(1, ND, start_t, 0)
    recv_t[b] = green[shift[shift[source]]]

    def arrive_b(u, carry):
        pltpu.make_async_copy(green.at[0], recv_d.at[u], sem_rd.at[u]).wait()

        @pl.when(u != b)
        def _():
            pltpu.make_async_copy(green.at[0], recv_t.at[u], sem_rt.at[u]).wait()

        return carry

    def pair_up(pair, carry):
        arrive_b(2 * pair, 0)
        arrive_b(2 * pair + 1, 0)
        even = recv_d[2 * pair].astype(F32)
        other = recv_d[2 * pair + 1].astype(F32)
        direct_re[pair] = jnp.where(left, even, swap(other))
        direct_im[pair] = jnp.where(left, swap(even), other)
        both = recv_t[pl.ds(2 * pair, 2)].astype(F32).reshape(2 * NF, PACK).T
        turned_re[pair, 16 : 16 + NF, :] = both[0:NF]
        turned_im[pair, 16 : 16 + NF, :] = both[NF:PACK]
        return carry

    lax.fori_loop(0, NM // 2, pair_up, 0)

    def copy_o(peer):
        return pltpu.make_async_remote_copy(
            src_ref=send_o.at[peer],
            dst_ref=recv_o.at[b],
            send_sem=sem_so.at[peer],
            recv_sem=sem_ro.at[b],
            device_id=(w, peer),
            device_id_type=MESH,
        )

    def window(i, carry):
        peer = lax.rem(b + i, ND)
        for k in range(2):
            offset = transfers[2 * peer + k]
            turn = (PACK + NQ // 2 - offset) & (PACK - 1)
            sum_re = jnp.zeros((NF, PACK), F32)
            sum_im = jnp.zeros((NF, PACK), F32)
            for pair in range(NM // 2):
                near_re = direct_re[pair]
                near_im = direct_im[pair]
                far_re = pltpu.roll(turned_re[pair, pl.ds(offset, NF), :], turn, 1)
                far_im = pltpu.roll(turned_im[pair, pl.ds(offset, NF), :], turn, 1)
                sum_re = sum_re + (near_re * far_re - near_im * far_im)
                sum_im = sum_im + (near_re * far_im + near_im * far_re)
            sum_re = sum_re + swap(sum_re)
            sum_im = sum_im + swap(sum_im)
            nu = offset - NQ // 2
            row = row_of + nu
            col = lane_of + nu
            keep = (row >= 0) & (row < NF) & (col >= 0) & (col < NF)
            send_o[peer, k] = jnp.where(keep, jnp.where(left, sum_re, sum_im), 0.0).astype(BF16)

        @pl.when(i < ND)
        def _():
            copy_o(peer).start()

        return carry

    lax.fori_loop(1, ND + 1, window, 0)
    recv_o[b] = send_o[b]

    def arrive_o(i, carry):
        peer = lax.rem(b + i, ND)
        pltpu.make_async_copy(send_o.at[peer], recv_o.at[peer], sem_ro.at[peer]).wait()
        return carry

    lax.fori_loop(1, ND, arrive_o, 0)

    for tile in range(NM // 2):
        even = recv_o[lax.rem(inverse[2 * tile] + w, ND)].astype(F32)
        other = recv_o[lax.rem(inverse[2 * tile + 1] + w, ND)].astype(F32)
        for k in range(2):
            out[0, k, :, tile * 128 : tile * 128 + 128] = jnp.where(left, even[k], swap(other[k]))
            out[1, k, :, tile * 128 : tile * 128 + 128] = jnp.where(left, swap(even[k]), other[k])

    def drain(i, carry):
        peer = lax.rem(b + i, ND)
        copy_t(peer).wait_send()
        copy_o(peer).wait_send()
        return carry

    lax.fori_loop(1, ND, drain, 0)

    def drain_d(m, carry):
        @pl.when(jnp.logical_not(is_own(m)))
        def _():
            copy_d(m).wait_send()

        return carry

    lax.fori_loop(0, NM, drain_d, 0)


def shards(vertex_times, vertex_sites, vertex_matrix, bare_green, transfer_momentum, transfers):
    vmem = pl.BlockSpec(memory_space=pltpu.VMEM)
    smem = pl.BlockSpec(memory_space=pltpu.SMEM)
    sems = pltpu.SemaphoreType.DMA((ND,))
    blocks = pltpu.VMEM((ND, NF, PACK), BF16)
    return pl.pallas_call(
        kernel,
        out_shape=jax.ShapeDtypeStruct((2, 2, NF, NV), F32),
        in_specs=[vmem, vmem, vmem, vmem, smem, smem],
        out_specs=vmem,
        scratch_shapes=[
            pltpu.VMEM((2, NF, NV), BF16),
            pltpu.VMEM((NM, PACK, NV), BF16),
            pltpu.VMEM((NV, PACK), F32),
            pltpu.VMEM((NV, PACK), F32),
            pltpu.SMEM((NM,), jnp.int32),
            blocks,
            pltpu.VMEM((NV, PACK), BF16),
            blocks,
            blocks,
            blocks,
            blocks,
            pltpu.VMEM((NM // 2, NF, PACK), F32),
            pltpu.VMEM((NM // 2, NF, PACK), F32),
            pltpu.VMEM((NM // 2, NF + 32, PACK), F32),
            pltpu.VMEM((NM // 2, NF + 32, PACK), F32),
            pltpu.VMEM((ND, 2, NF, PACK), BF16),
            pltpu.VMEM((ND, 2, NF, PACK), BF16),
        ]
        + [sems] * 8,
        compiler_params=pltpu.CompilerParams(collective_id=0, has_side_effects=True),
    )(vertex_times, vertex_sites, vertex_matrix, bare_green, transfer_momentum, transfers)


def solution(mesh):
    return jax.shard_map(
        shards,
        mesh=mesh,
        in_specs=(P("blk", None), P("blk", None), P("blk", "walk", None), P(), P(), P()),
        out_specs=P(None, "blk", "walk", None),
        check_vma=False,
    )
```

time: 331 us -> 48.7 us (0.15)
  waiting for transfers between devices: 139 us -> 0 us
  other arithmetic: 87.8 us -> 0 us
  Pallas kernels: 0 us -> 46.3 us
  local copies, waits for them, and re-layouts: 41.1 us -> 2.31 us
  matrix products: 38.4 us -> 0 us
  between operations: 14.8 us -> 0.01 us
  starting transfers between devices: 4.11 us -> 0 us
    all_gather x3 -> x0, waiting for transfers between devices: 127 us -> none  [the longest x1 66.4 us: shards(): piece = lax.all_gather(vertex_matrix[0], 'walk', axis=0, tiled=True)]
    convert_element_type x49 -> x0, other arithmetic: 57.5 us -> none  [the longest x1 20.1 us: fourier_table(): jnp.cos(angle).astype(jnp.bfloat16)]
    pallas_call x0 -> x1, Pallas kernels: none -> 46.3 us  [shards(): pl.pallas_call(kernel, out_shape=jax.ShapeDtypeStruct((2, 2, NF, NV), F32...]
    dot_general x6 -> x0, matrix products: 38.4 us -> none  [the longest x4 34.8 us: product(): lax.dot_general(left, right, contract, preferred_element_type=jnp.float32)]
    slice x114 -> x0, local copies, waits for them, and re-layouts: 24.2 us -> none  [the longest x96 13.4 us: accumulate(): part_re = near[0] * shifted[0] - near[1] * shifted[1]]
    and x49 -> x0, other arithmetic: 21.6 us -> none  [the longest x16 19.1 us: accumulate(): valid = (spots + offset >= 0) & (spots + offset < NF)]
    all_to_all x1 -> x0, waiting for transfers between devices: 11 us -> none  [shards(): lax.all_to_all(outgoing, 'walk', split_axis=3, concat_axis=2, tiled=True)]
    reshape x19 -> x0, local copies, waits for them, and re-layouts: 7.19 us -> none  [the longest x16 5.45 us: accumulate(): grid = turned.reshape(2, moments, NF, NM, NF)]
  transfers between devices with their start and end apart: 4 -> 0, of which waited for: 4 -> 0; matrix products, arithmetic and copies ran while one was open for 9% -> 0% of each run, Pallas kernels for 0% -> 0%
where the time goes in v1:
time: 48.7 us; the launch traced here: 48.6 us
  Pallas kernels  46.3 us (95%)
  local copies, waits for them, and re-layouts  2.31 us (5%)
    pallas_call x1, Pallas kernels, shards(): pl.pallas_call(kernel, out_shape=jax.ShapeDtypeStruct((2, 2, NF, NV), F32...  46.3 us
    unnamed x1, local copies, waits for them, and re-layouts  2.31 us

profile of v1, /device:TPU:1, one launch (start us, length us, event | category | flops | bytes accessed | tf_op | source)
XLA Modules:
  0.0 48.6 jit_solution(9487203936851237663)
XLA Ops:
  0.0 46.3 %shard_map.64 = f32[2,2,64,1024]{3,2,1,0:T(8,128)} custom-call(s32[1,1024]{1,0:T(1,128)} %times.1, s32[1,1024]{1,0:T(1,128)} %sites.1, bf16[1,64,1024]{2,1,0:T(8,128)(2,1)} %matrix.1, f32[2,1024]{1,0:T(2,128)} %bare.1, s32[16]{0:T(128)} %shift.1, s32[32]{0:T(128)} %transfers.1), custom_call_target="tpu_custom_call" | custom-call | tf_op jit(solution)/shard_map/pallas_call | solution.py:363
  46.3 2.3 %copy.8 = f32[2,2,64,1024]{3,2,1,0:T(8,128)} copy(f32[2,2,64,1024]{3,2,1,0:T(8,128)} %shard_map.64) | data formatting | bytes 2097152

commit v2 on v1

--- a/solution.py
+++ b/solution.py
@@ -78,8 +78,19 @@
     w = lax.axis_index("walk")
     b = lax.axis_index("blk")
     source = lax.rem(b - w + ND, ND)
-    twice = lax.rem(2 * w, ND)
-    alone = twice == b
+    alone = source == w
+
+    def along_walk(i):
+        step = i // 2
+        far = (step + 1) // 2
+        z = w // 2 + 4 + far - 2 * far * (step % 2)
+        return lax.rem(z + 8, 8) * 2 + lax.rem(w + i + 1, 2)
+
+    def along_blk(i):
+        step = i // 4
+        y = (b // 2) % 4 + jnp.where(step == 0, 2, jnp.where(step == 1, 1, jnp.where(step == 2, 3, 0)))
+        x = b // 8 + 1 - (i % 4) // 2
+        return lax.rem(x, 2) * 8 + lax.rem(y, 4) * 2 + lax.rem(b + i + 1, 2)
 
     barrier = pltpu.get_barrier_semaphore()
 
@@ -89,15 +100,6 @@
         return carry
 
     lax.fori_loop(1, ND, greet, 0)
-
-    def greet_source(i, carry):
-        @pl.when(jnp.logical_not(jnp.logical_and(alone, i == b)))
-        def _():
-            pl.semaphore_signal(barrier, inc=1, device_id=(source, i), device_id_type=MESH)
-
-        return carry
-
-    lax.fori_loop(0, ND, greet_source, 0)
 
     def base_rows(i, carry):
         first = pl.multiple_of(i * 16, 16)
@@ -133,7 +135,7 @@
 
     lax.fori_loop(0, ND, project, 0)
 
-    pl.semaphore_wait(barrier, 3 * ND - 2 - alone.astype(jnp.int32))
+    pl.semaphore_wait(barrier, 2 * ND - 2)
 
     def copy_a(peer):
         return pltpu.make_async_remote_copy(
@@ -146,10 +148,10 @@
         )
 
     def start_a(i, carry):
-        copy_a(lax.rem(w + i, ND)).start()
-        return carry
-
-    lax.fori_loop(1, ND, start_a, 0)
+        copy_a(along_walk(i)).start()
+        return carry
+
+    lax.fori_loop(0, ND - 1, start_a, 0)
     recv_a[pl.ds(pl.multiple_of(w * NF, NF), NF), :] = send_a[w]
 
     for part, target in ((0, outer_re), (1, outer_im)):
@@ -214,19 +216,17 @@
         return jnp.logical_and(alone, m == w)
 
     def assemble(group, carry):
-        first = group * 4
-        rows = table[pl.ds(first, 4)].reshape(4 * PACK, NV)
+        momenta = [4 * group + k for k in range(4)]
+        rows = jnp.concatenate([table[m] for m in momenta], axis=0)
         raw = jnp.dot(rows, recv_a[...], preferred_element_type=F32)
-        for k in range(4):
-            m = first + k
+        for k, m in enumerate(momenta):
             spread = raw[k * PACK : k * PACK + NF] * minus_right + swap(raw[k * PACK + NF : (k + 1) * PACK])
             part = spread * col_re + swap(spread) * col_im
             part = part + jnp.where(jnp.logical_and(left, row_of == lane_of), (mine == m).astype(F32), 0.0)
             start = pl.multiple_of(m * NF, NF)
             value = outer_re[pl.ds(start, NF), :] * part + outer_im[pl.ds(start, NF), :] * minus_left * swap(part)
             green[m] = value.astype(BF16)
-        for k in range(4):
-            m = first + k
+        for m in momenta:
 
             @pl.when(jnp.logical_not(is_own(m)))
             def _():
@@ -251,12 +251,12 @@
         )
 
     def start_t(i, carry):
-        peer = lax.rem(b + i, ND)
+        peer = along_blk(i)
         send_t[peer] = green[shift[shift[lax.rem(peer - w + ND, ND)]]]
         copy_t(peer).start()
         return carry
 
-    lax.fori_loop(1, ND, start_t, 0)
+    lax.fori_loop(0, ND - 1, start_t, 0)
     recv_t[b] = green[shift[shift[source]]]
 
     def arrive_b(u, carry):
@@ -293,7 +293,7 @@
         )
 
     def window(i, carry):
-        peer = lax.rem(b + i, ND)
+        peer = along_blk(i)
         for k in range(2):
             offset = transfers[2 * peer + k]
             turn = (PACK + NQ // 2 - offset) & (PACK - 1)
@@ -314,13 +314,13 @@
             keep = (row >= 0) & (row < NF) & (col >= 0) & (col < NF)
             send_o[peer, k] = jnp.where(keep, jnp.where(left, sum_re, sum_im), 0.0).astype(BF16)
 
-        @pl.when(i < ND)
+        @pl.when(i < ND - 1)
         def _():
             copy_o(peer).start()
 
         return carry
 
-    lax.fori_loop(1, ND + 1, window, 0)
+    lax.fori_loop(0, ND, window, 0)
     recv_o[b] = send_o[b]
 
     def arrive_o(i, carry):

time: 48.7 us -> 46.7 us (0.959)
  Pallas kernels: 46.3 us -> 44.2 us
    pallas_call x1, Pallas kernels: 46.3 us -> 44.2 us  [shards(): pl.pallas_call(kernel, out_shape=jax.ShapeDtypeStruct((2, 2, NF, NV), F32...]
where the time goes in v2:
time: 46.7 us; the launch traced here: 46.6 us
  Pallas kernels  44.2 us (95%)
  local copies, waits for them, and re-layouts  2.31 us (5%)
    pallas_call x1, Pallas kernels, shards(): pl.pallas_call(kernel, out_shape=jax.ShapeDtypeStruct((2, 2, NF, NV), F32...  44.2 us
    unnamed x1, local copies, waits for them, and re-layouts  2.31 us

profile of v2, /device:TPU:1, one launch (start us, length us, event | category | flops | bytes accessed | tf_op | source)
XLA Modules:
  0.0 46.6 jit_solution(7321834195939603864)
XLA Ops:
  0.0 44.2 %shard_map.64 = f32[2,2,64,1024]{3,2,1,0:T(8,128)} custom-call(s32[1,1024]{1,0:T(1,128)} %times.1, s32[1,1024]{1,0:T(1,128)} %sites.1, bf16[1,64,1024]{2,1,0:T(8,128)(2,1)} %matrix.1, f32[2,1024]{1,0:T(2,128)} %bare.1, s32[16]{0:T(128)} %shift.1, s32[32]{0:T(128)} %transfers.1), custom_call_target="tpu_custom_call" | custom-call | tf_op jit(solution)/shard_map/pallas_call | solution.py:363
  44.3 2.3 %copy.8 = f32[2,2,64,1024]{3,2,1,0:T(8,128)} copy(f32[2,2,64,1024]{3,2,1,0:T(8,128)} %shard_map.64) | data formatting | bytes 2097152

commit v3 on v2

--- a/solution.py
+++ b/solution.py
@@ -17,6 +17,7 @@
 PACK = 2 * NF
 TURN = 8 * NT
 QUARTER = TURN // 4
+BAND = 16
 MESH = pl.DeviceIdType.MESH
 F32 = jnp.float32
 BF16 = jnp.bfloat16
@@ -37,26 +38,39 @@
     return jnp.where(odd, -sine, cosine) * sign, jnp.where(odd, cosine, sine) * sign
 
 
+def pick(value, lanes):
+    return jnp.take_along_axis(value, lanes, axis=1)
+
+
 def swap(value):
     return pltpu.roll(value, NF, 1)
 
 
 def kernel(
+    times_in,
+    sites_in,
+    matrix_in,
+    bare_in,
+    shift_in,
+    transfers_in,
+    out,
+    inverse,
     times,
     sites,
     matrix,
     bare,
     shift,
     transfers,
-    out,
     base,
     table,
     outer_re,
     outer_im,
-    inverse,
+    tables,
+    chosen,
     send_a,
     recv_a,
     green,
+    send_d,
     send_t,
     recv_d,
     recv_t,
@@ -64,8 +78,9 @@
     direct_im,
     turned_re,
     turned_im,
+    total,
     send_o,
-    recv_o,
+    sem_in,
     sem_sa,
     sem_ra,
     sem_sd,
@@ -101,6 +116,24 @@
 
     lax.fori_loop(1, ND, greet, 0)
 
+    incoming = [
+        pltpu.make_async_copy(held, here, sem_in.at[k])
+        for k, (held, here) in enumerate(
+            (
+                (times_in, times),
+                (sites_in, sites),
+                (matrix_in, matrix),
+                (bare_in, bare),
+                (shift_in, shift),
+                (transfers_in, transfers),
+            )
+        )
+    ]
+    for copy in incoming:
+        copy.start()
+    for copy in incoming:
+        copy.wait()
+
     def base_rows(i, carry):
         first = pl.multiple_of(i * 16, 16)
         f = lax.broadcasted_iota(jnp.int32, (16, NV), 0) + first
@@ -126,11 +159,25 @@
 
     lax.fori_loop(0, NM, rotate, 0)
 
+    left = lax.broadcasted_iota(jnp.int32, (NF, PACK), 1) < NF
+    row_of = lax.broadcasted_iota(jnp.int32, (NF, PACK), 0)
+    whole_lane = lax.broadcasted_iota(jnp.int32, (NF, PACK), 1)
+    lane_of = whole_lane & (NF - 1)
+    skew = (whole_lane & NF) | ((whole_lane + row_of) & (NF - 1))
+    straight = (whole_lane & NF) | ((whole_lane - row_of) & (NF - 1))
+    minus_left = jnp.where(left, -1.0, 1.0)
+    scale = NV ** (-0.5)
+
+    for m in range(NM):
+        for part in range(2):
+            piece = bare[part : part + 1, m * NF : m * NF + NF]
+            tables[m, part : part + 1, :] = jnp.concatenate([piece, -piece if part == 0 else piece], axis=1) * scale
+
     def project(i, carry):
-        block = lax.dot_general(
-            matrix[0], table[shift[i]], (((1,), (1,)), ((), ())), preferred_element_type=F32
-        )
-        send_a[i] = block.astype(BF16)
+        m = shift[i]
+        block = lax.dot_general(matrix[0], table[m], (((1,), (1,)), ((), ())), preferred_element_type=F32)
+        factors = tables[m]
+        send_a[i] = (block * factors[0:1] + swap(block) * factors[1:2]).astype(BF16)
         return carry
 
     lax.fori_loop(0, ND, project, 0)
@@ -157,7 +204,10 @@
     for part, target in ((0, outer_re), (1, outer_im)):
         for tile in range(NV // 128):
             row = jnp.broadcast_to(bare[part : part + 1, tile * 128 : tile * 128 + 128], (128, 128))
-            target[tile * 128 : tile * 128 + 128, :] = row.T
+            column = row.T
+            if part == 1:
+                column = jnp.where(lax.broadcasted_iota(jnp.int32, (128, 128), 1) < NF, -column, column)
+            target[tile * 128 : tile * 128 + 128, :] = column
 
     for m in range(NM):
         position = jnp.int32(0)
@@ -170,20 +220,9 @@
             target[pair, 0:16, :] = jnp.zeros((16, 128), F32)
             target[pair, 80:96, :] = jnp.zeros((16, 128), F32)
 
-    left = lax.broadcasted_iota(jnp.int32, (NF, PACK), 1) < NF
-    row_of = lax.broadcasted_iota(jnp.int32, (NF, PACK), 0)
-    lane_of = lax.broadcasted_iota(jnp.int32, (NF, PACK), 1) & (NF - 1)
-    minus_right = jnp.where(left, 1.0, -1.0)
-    minus_left = -minus_right
     mine = shift[w]
-    col_re = bare[0:1, 0:NF]
-    col_im = bare[1:2, 0:NF]
-    for m in range(1, NM):
-        col_re = jnp.where(mine == m, bare[0:1, m * NF : m * NF + NF], col_re)
-        col_im = jnp.where(mine == m, bare[1:2, m * NF : m * NF + NF], col_im)
-    scale = NV ** (-0.5)
-    col_re = jnp.concatenate([col_re, col_re], axis=1) * scale
-    col_im = jnp.concatenate([-col_im, col_im], axis=1) * scale
+    for i in range(ND):
+        chosen[i] = shift[shift[lax.rem(along_blk(i) - w + ND, ND)]]
 
     def arrive_a(i, carry):
         peer = lax.rem(w + i, ND)
@@ -201,7 +240,7 @@
 
     def copy_d(m):
         return pltpu.make_async_remote_copy(
-            src_ref=green.at[m],
+            src_ref=send_d.at[m],
             dst_ref=recv_d.at[b],
             send_sem=sem_sd.at[m],
             recv_sem=sem_rd.at[b],
@@ -210,22 +249,24 @@
         )
 
     def own_d(m):
-        return pltpu.make_async_copy(green.at[m], recv_d.at[b], sem_rd.at[b])
+        return pltpu.make_async_copy(send_d.at[m], recv_d.at[b], sem_rd.at[b])
 
     def is_own(m):
         return jnp.logical_and(alone, m == w)
+
+    diagonal = jnp.where(jnp.logical_and(left, row_of == lane_of), 1.0, 0.0)
 
     def assemble(group, carry):
         momenta = [4 * group + k for k in range(4)]
         rows = jnp.concatenate([table[m] for m in momenta], axis=0)
         raw = jnp.dot(rows, recv_a[...], preferred_element_type=F32)
         for k, m in enumerate(momenta):
-            spread = raw[k * PACK : k * PACK + NF] * minus_right + swap(raw[k * PACK + NF : (k + 1) * PACK])
-            part = spread * col_re + swap(spread) * col_im
-            part = part + jnp.where(jnp.logical_and(left, row_of == lane_of), (mine == m).astype(F32), 0.0)
+            part = raw[k * PACK : k * PACK + NF] + swap(raw[k * PACK + NF : (k + 1) * PACK]) * minus_left
+            part = part + diagonal * (mine == m).astype(F32)
             start = pl.multiple_of(m * NF, NF)
-            value = outer_re[pl.ds(start, NF), :] * part + outer_im[pl.ds(start, NF), :] * minus_left * swap(part)
+            value = outer_re[pl.ds(start, NF), :] * part + outer_im[pl.ds(start, NF), :] * swap(part)
             green[m] = value.astype(BF16)
+            send_d[m] = pick(value, skew).astype(BF16)
         for m in momenta:
 
             @pl.when(jnp.logical_not(is_own(m)))
@@ -252,12 +293,12 @@
 
     def start_t(i, carry):
         peer = along_blk(i)
-        send_t[peer] = green[shift[shift[lax.rem(peer - w + ND, ND)]]]
+        send_t[peer] = green[chosen[i]]
         copy_t(peer).start()
         return carry
 
     lax.fori_loop(0, ND - 1, start_t, 0)
-    recv_t[b] = green[shift[shift[source]]]
+    recv_t[b] = green[chosen[ND - 1]]
 
     def arrive_b(u, carry):
         pltpu.make_async_copy(green.at[0], recv_d.at[u], sem_rd.at[u]).wait()
@@ -276,8 +317,8 @@
         direct_re[pair] = jnp.where(left, even, swap(other))
         direct_im[pair] = jnp.where(left, swap(even), other)
         both = recv_t[pl.ds(2 * pair, 2)].astype(F32).reshape(2 * NF, PACK).T
-        turned_re[pair, 16 : 16 + NF, :] = both[0:NF]
-        turned_im[pair, 16 : 16 + NF, :] = both[NF:PACK]
+        turned_re[pair, 16 : 16 + NF, :] = pick(both[0:NF], skew)
+        turned_im[pair, 16 : 16 + NF, :] = pick(both[NF:PACK], skew)
         return carry
 
     lax.fori_loop(0, NM // 2, pair_up, 0)
@@ -285,34 +326,45 @@
     def copy_o(peer):
         return pltpu.make_async_remote_copy(
             src_ref=send_o.at[peer],
-            dst_ref=recv_o.at[b],
+            dst_ref=out.at[source],
             send_sem=sem_so.at[peer],
-            recv_sem=sem_ro.at[b],
+            recv_sem=sem_ro.at[source],
             device_id=(w, peer),
             device_id_type=MESH,
         )
 
     def window(i, carry):
         peer = along_blk(i)
+        offsets = [transfers[2 * peer + k] for k in range(2)]
+
+        def multiply(step, carry):
+            first = pl.multiple_of(step * BAND, BAND)
+            band = pl.ds(first, BAND)
+            sums = [[jnp.zeros((BAND, PACK), F32)] * 2 for k in range(2)]
+            for pair in range(NM // 2):
+                near_re = direct_re[pair, band]
+                near_im = direct_im[pair, band]
+                for k in range(2):
+                    far_re = turned_re[pair, pl.ds(offsets[k] + first, BAND), :]
+                    far_im = turned_im[pair, pl.ds(offsets[k] + first, BAND), :]
+                    sums[k] = [
+                        sums[k][0] + (near_re * far_re - near_im * far_im),
+                        sums[k][1] + (near_re * far_im + near_im * far_re),
+                    ]
+            for k in range(2):
+                total[2 * k, band] = sums[k][0]
+                total[2 * k + 1, band] = sums[k][1]
+            return carry
+
+        lax.fori_loop(0, NF // BAND, multiply, 0)
         for k in range(2):
-            offset = transfers[2 * peer + k]
-            turn = (PACK + NQ // 2 - offset) & (PACK - 1)
-            sum_re = jnp.zeros((NF, PACK), F32)
-            sum_im = jnp.zeros((NF, PACK), F32)
-            for pair in range(NM // 2):
-                near_re = direct_re[pair]
-                near_im = direct_im[pair]
-                far_re = pltpu.roll(turned_re[pair, pl.ds(offset, NF), :], turn, 1)
-                far_im = pltpu.roll(turned_im[pair, pl.ds(offset, NF), :], turn, 1)
-                sum_re = sum_re + (near_re * far_re - near_im * far_im)
-                sum_im = sum_im + (near_re * far_im + near_im * far_re)
-            sum_re = sum_re + swap(sum_re)
-            sum_im = sum_im + swap(sum_im)
-            nu = offset - NQ // 2
+            sum_re, sum_im = [value + swap(value) for value in (total[2 * k], total[2 * k + 1])]
+            nu = offsets[k] - NQ // 2
             row = row_of + nu
             col = lane_of + nu
             keep = (row >= 0) & (row < NF) & (col >= 0) & (col < NF)
-            send_o[peer, k] = jnp.where(keep, jnp.where(left, sum_re, sum_im), 0.0).astype(BF16)
+            result = pick(jnp.where(left, sum_re, sum_im), straight)
+            send_o[peer, k] = jnp.where(keep, result, 0.0).astype(BF16)
 
         @pl.when(i < ND - 1)
         def _():
@@ -321,21 +373,14 @@
         return carry
 
     lax.fori_loop(0, ND, window, 0)
-    recv_o[b] = send_o[b]
+    own_o = pltpu.make_async_copy(send_o.at[b], out.at[source], sem_ro.at[source])
+    own_o.start()
 
     def arrive_o(i, carry):
-        peer = lax.rem(b + i, ND)
-        pltpu.make_async_copy(send_o.at[peer], recv_o.at[peer], sem_ro.at[peer]).wait()
-        return carry
-
-    lax.fori_loop(1, ND, arrive_o, 0)
-
-    for tile in range(NM // 2):
-        even = recv_o[lax.rem(inverse[2 * tile] + w, ND)].astype(F32)
-        other = recv_o[lax.rem(inverse[2 * tile + 1] + w, ND)].astype(F32)
-        for k in range(2):
-            out[0, k, :, tile * 128 : tile * 128 + 128] = jnp.where(left, even[k], swap(other[k]))
-            out[1, k, :, tile * 128 : tile * 128 + 128] = jnp.where(left, swap(even[k]), other[k])
+        pltpu.make_async_copy(send_o.at[i], out.at[i], sem_ro.at[i]).wait()
+        return carry
+
+    lax.fori_loop(0, ND, arrive_o, 0)
 
     def drain(i, carry):
         peer = lax.rem(b + i, ND)
@@ -355,21 +400,44 @@
     lax.fori_loop(0, NM, drain_d, 0)
 
 
+def spread_out(inverse, blocks, out):
+    left = lax.broadcasted_iota(jnp.int32, (NF, PACK), 1) < NF
+    for tile in range(NM // 2):
+        even = blocks[inverse[2 * tile]].astype(F32)
+        other = blocks[inverse[2 * tile + 1]].astype(F32)
+        for k in range(2):
+            out[0, k, :, tile * 128 : tile * 128 + 128] = jnp.where(left, even[k], swap(other[k]))
+            out[1, k, :, tile * 128 : tile * 128 + 128] = jnp.where(left, swap(even[k]), other[k])
+
+
 def shards(vertex_times, vertex_sites, vertex_matrix, bare_green, transfer_momentum, transfers):
     vmem = pl.BlockSpec(memory_space=pltpu.VMEM)
     smem = pl.BlockSpec(memory_space=pltpu.SMEM)
+    here = pl.BlockSpec(memory_space=pl.ANY)
     sems = pltpu.SemaphoreType.DMA((ND,))
     blocks = pltpu.VMEM((ND, NF, PACK), BF16)
-    return pl.pallas_call(
+    pairs = pltpu.VMEM((NM // 2, NF, PACK), F32)
+    padded = pltpu.VMEM((NM // 2, NF + 32, PACK), F32)
+    results, inverse = pl.pallas_call(
         kernel,
-        out_shape=jax.ShapeDtypeStruct((2, 2, NF, NV), F32),
-        in_specs=[vmem, vmem, vmem, vmem, smem, smem],
-        out_specs=vmem,
+        out_shape=[
+            jax.ShapeDtypeStruct((ND, 2, NF, PACK), BF16),
+            jax.ShapeDtypeStruct((NM,), jnp.int32),
+        ],
+        in_specs=[here] * 6,
+        out_specs=[here, smem],
         scratch_shapes=[
+            pltpu.VMEM((1, NV), jnp.int32),
+            pltpu.VMEM((1, NV), jnp.int32),
+            pltpu.VMEM((1, NF, NV), BF16),
+            pltpu.VMEM((2, NV), F32),
+            pltpu.SMEM((NM,), jnp.int32),
+            pltpu.SMEM((NQ,), jnp.int32),
             pltpu.VMEM((2, NF, NV), BF16),
             pltpu.VMEM((NM, PACK, NV), BF16),
             pltpu.VMEM((NV, PACK), F32),
             pltpu.VMEM((NV, PACK), F32),
+            pltpu.VMEM((NM, 8, PACK), F32),
             pltpu.SMEM((NM,), jnp.int32),
             blocks,
             pltpu.VMEM((NV, PACK), BF16),
@@ -377,16 +445,24 @@
             blocks,
             blocks,
             blocks,
-            pltpu.VMEM((NM // 2, NF, PACK), F32),
-            pltpu.VMEM((NM // 2, NF, PACK), F32),
-            pltpu.VMEM((NM // 2, NF + 32, PACK), F32),
-            pltpu.VMEM((NM // 2, NF + 32, PACK), F32),
+            blocks,
+            pairs,
+            pairs,
+            padded,
+            padded,
+            pltpu.VMEM((4, NF, PACK), F32),
             pltpu.VMEM((ND, 2, NF, PACK), BF16),
-            pltpu.VMEM((ND, 2, NF, PACK), BF16),
+            pltpu.SemaphoreType.DMA((6,)),
         ]
         + [sems] * 8,
         compiler_params=pltpu.CompilerParams(collective_id=0, has_side_effects=True),
     )(vertex_times, vertex_sites, vertex_matrix, bare_green, transfer_momentum, transfers)
+    return pl.pallas_call(
+        spread_out,
+        out_shape=jax.ShapeDtypeStruct((2, 2, NF, NV), F32),
+        in_specs=[smem, vmem],
+        out_specs=vmem,
+    )(inverse, results)
 
 
 def solution(mesh):

time: 46.7 us -> 46.3 us (level)
  local copies, waits for them, and re-layouts: 2.31 us -> 0 us
  Pallas kernels: 44.2 us -> 46.2 us
    unnamed x1 -> x0, local copies, waits for them, and re-layouts: 2.31 us -> none
    pallas_call x1 -> x2, Pallas kernels: 44.2 us -> 46.2 us  [the longest x1 43.9 us: shards(): pl.pallas_call(kernel, out_shape=[jax.ShapeDtypeStruct((ND, 2, NF, PACK),...]
where the time goes in v3:
time: 46.3 us; the launch traced here: 46.2 us
  Pallas kernels  46.2 us (100%)
    pallas_call x1, Pallas kernels, shards(): pl.pallas_call(kernel, out_shape=[jax.ShapeDtypeStruct((ND, 2, NF, PACK),...  43.9 us
    pallas_call x1, Pallas kernels, shards(): pl.pallas_call(spread_out, out_shape=jax.ShapeDtypeStruct((2, 2, NF, NV),...  2.26 us

profile of v3, /device:TPU:1, one launch (start us, length us, event | category | flops | bytes accessed | tf_op | source)
XLA Modules:
  0.0 46.2 jit_solution(17830944278318900355)
XLA Ops:
  0.0 43.9 %shard_map.64 = (bf16[16,2,64,128]{3,2,1,0:T(8,128)(2,1)}, s32[16]{0:T(128)}) custom-call(s32[1,1024]{1,0:T(1,128)} %times_in.1, s32[1,1024]{1,0:T(1,128)} %sites_in.1, bf16[1,64,1024]{2,1,0:T(8,128)(2,1)} %matrix_in.1, f32[2,1024]{1,0:T(2,128)} %bare_in.1, s32[16]{0:T(128)} %shift_in.1, s32[32]{0:T(128)} %transfers_in.1), custom_call_target="tpu_custom_call" | custom-call | tf_op jit(solution)/shard_map/pallas_call | solution.py:421
  43.9 2.3 %shard_map.65 = f32[2,2,64,1024]{3,2,1,0:T(8,128)} custom-call(s32[16]{0:T(128)} %get-tuple-element.7.inverse, bf16[16,2,64,128]{3,2,1,0:T(8,128)(2,1)} %get-tuple-element.8.blocks), custom_call_target="tpu_custom_call" | custom-call | tf_op jit(solution)/shard_map/pallas_call | solution.py:460

commit v4 on v3

--- a/solution.py
+++ b/solution.py
@@ -61,14 +61,17 @@
     bare,
     shift,
     transfers,
+    factor,
     base,
+    partial,
+    projected,
     table,
     outer_re,
     outer_im,
-    tables,
     chosen,
     send_a,
     recv_a,
+    held,
     green,
     send_d,
     send_t,
@@ -92,29 +95,19 @@
 ):
     w = lax.axis_index("walk")
     b = lax.axis_index("blk")
-    source = lax.rem(b - w + ND, ND)
+    source = (b - w) & (ND - 1)
     alone = source == w
 
     def along_walk(i):
-        step = i // 2
-        far = (step + 1) // 2
-        z = w // 2 + 4 + far - 2 * far * (step % 2)
-        return lax.rem(z + 8, 8) * 2 + lax.rem(w + i + 1, 2)
+        z = (w >> 1) + (4, 3, 5, 2, 6, 1, 7, 0)[i // 2]
+        return ((z & 7) << 1) + ((w + i + 1) & 1)
 
     def along_blk(i):
-        step = i // 4
-        y = (b // 2) % 4 + jnp.where(step == 0, 2, jnp.where(step == 1, 1, jnp.where(step == 2, 3, 0)))
-        x = b // 8 + 1 - (i % 4) // 2
-        return lax.rem(x, 2) * 8 + lax.rem(y, 4) * 2 + lax.rem(b + i + 1, 2)
+        y = (b >> 1) + (2, 1, 3, 0)[i // 4]
+        x = (b >> 3) + 1 - (i % 4) // 2
+        return ((x & 1) << 3) + ((y & 3) << 1) + ((b + i + 1) & 1)
 
     barrier = pltpu.get_barrier_semaphore()
-
-    def greet(i, carry):
-        pl.semaphore_signal(barrier, inc=1, device_id=(lax.rem(w + i, ND), b), device_id_type=MESH)
-        pl.semaphore_signal(barrier, inc=1, device_id=(w, lax.rem(b + i, ND)), device_id_type=MESH)
-        return carry
-
-    lax.fori_loop(1, ND, greet, 0)
 
     incoming = [
         pltpu.make_async_copy(held, here, sem_in.at[k])
@@ -131,33 +124,27 @@
     ]
     for copy in incoming:
         copy.start()
+    for i in range(ND - 1):
+        pl.semaphore_signal(barrier, inc=1, device_id=(along_walk(i), b), device_id_type=MESH)
+        pl.semaphore_signal(barrier, inc=1, device_id=(w, along_blk(i)), device_id_type=MESH)
     for copy in incoming:
         copy.wait()
 
-    def base_rows(i, carry):
-        first = pl.multiple_of(i * 16, 16)
-        f = lax.broadcasted_iota(jnp.int32, (16, NV), 0) + first
-        phase = (4 * (2 * f + 1 - NF) * times[...]) & (TURN - 1)
-        cosine, sine = sincos(phase)
-        base[0, pl.ds(first, 16), :] = cosine.astype(BF16)
-        base[1, pl.ds(first, 16), :] = sine.astype(BF16)
-        return carry
-
-    lax.fori_loop(0, NF // 16, base_rows, 0)
-
-    def rotate(m, carry):
-        turn = ((m // SIDE) * (sites[...] >> 2) + (m % SIDE) * (sites[...] & 3)) & 3
-        sign = (1 - (turn & 2)).astype(F32)
-        odd = (turn & 1).astype(F32)
-        along = jnp.broadcast_to((1.0 - odd) * sign, (NF, NV)).astype(BF16)
-        across = jnp.broadcast_to(odd * sign, (NF, NV)).astype(BF16)
-        cosine = base[0]
-        sine = base[1]
-        table[m, 0:NF, :] = cosine * along + sine * across
-        table[m, NF:PACK, :] = sine * along - cosine * across
-        return carry
-
-    lax.fori_loop(0, NM, rotate, 0)
+    step = lax.broadcasted_iota(jnp.int32, (16, NV), 0)
+    step = jnp.where(step < 8, 64 * step, 8 * (step - 8) + 4 * (1 - NF))
+    cosine, sine = sincos((step * times[...]) & (TURN - 1))
+    factor[0] = cosine
+    factor[1] = sine
+    fine_cos = factor[0, 8:16, :]
+    fine_sin = factor[1, 8:16, :]
+    for g in range(0, 8, 2):
+        coarse = [(factor[0, g + k : g + k + 1, :], factor[1, g + k : g + k + 1, :]) for k in range(2)]
+        base[8 * g : 8 * g + 16, :] = jnp.concatenate(
+            [c * fine_cos - n * fine_sin for c, n in coarse], axis=0
+        ).astype(BF16)
+        base[NF + 8 * g : NF + 8 * g + 16, :] = jnp.concatenate(
+            [n * fine_cos + c * fine_sin for c, n in coarse], axis=0
+        ).astype(BF16)
 
     left = lax.broadcasted_iota(jnp.int32, (NF, PACK), 1) < NF
     row_of = lax.broadcasted_iota(jnp.int32, (NF, PACK), 0)
@@ -168,38 +155,69 @@
     minus_left = jnp.where(left, -1.0, 1.0)
     scale = NV ** (-0.5)
 
-    for m in range(NM):
-        for part in range(2):
-            piece = bare[part : part + 1, m * NF : m * NF + NF]
-            tables[m, part : part + 1, :] = jnp.concatenate([piece, -piece if part == 0 else piece], axis=1) * scale
-
-    def project(i, carry):
-        m = shift[i]
-        block = lax.dot_general(matrix[0], table[m], (((1,), (1,)), ((), ())), preferred_element_type=F32)
-        factors = tables[m]
-        send_a[i] = (block * factors[0:1] + swap(block) * factors[1:2]).astype(BF16)
-        return carry
-
-    lax.fori_loop(0, ND, project, 0)
+    def quarter(block):
+        return -minus_left * swap(block)
+
+    def turns(blocks):
+        even, odd = blocks[0] + blocks[2], blocks[1] + blocks[3]
+        apart, turned = blocks[0] - blocks[2], quarter(blocks[1] - blocks[3])
+        return even + odd, apart + turned, even - odd, apart - turned
+
+    for x in range(SIDE):
+        rows = []
+        for y in range(SIDE):
+            here = jnp.where(sites[...] == SIDE * x + y, 1.0, 0.0)
+            rows.append(matrix[0] * jnp.broadcast_to(here, (NF, NV)).astype(BF16))
+        block = lax.dot_general(
+            jnp.concatenate(rows, axis=0), base[...], (((1,), (1,)), ((), ())), preferred_element_type=F32
+        )
+        for y, value in enumerate(turns([block[NF * y : NF * y + NF] for y in range(SIDE)])):
+            partial[SIDE * x + y] = value
+    for y in range(SIDE):
+        for x, value in enumerate(turns([partial[SIDE * x + y] for x in range(SIDE)])):
+            m = SIDE * x + y
+            piece_re = bare[0:1, m * NF : m * NF + NF] * scale
+            piece_im = bare[1:2, m * NF : m * NF + NF] * scale
+            value = value * jnp.concatenate([piece_re, -piece_re], axis=1) + swap(value) * jnp.concatenate(
+                [piece_im, piece_im], axis=1
+            )
+            projected[m] = value.astype(BF16)
+    for i in range(ND):
+        send_a[i] = projected[shift[along_walk(i)]]
 
     pl.semaphore_wait(barrier, 2 * ND - 2)
 
-    def copy_a(peer):
+    def rows_from(peer):
+        return recv_a.at[pl.ds(pl.multiple_of(peer * NF, NF), NF)]
+
+    def copy_a(i):
+        peer = along_walk(i)
         return pltpu.make_async_remote_copy(
-            src_ref=send_a.at[peer],
-            dst_ref=recv_a.at[pl.ds(pl.multiple_of(w * NF, NF), NF)],
-            send_sem=sem_sa.at[peer],
+            src_ref=send_a.at[i],
+            dst_ref=rows_from(w),
+            send_sem=sem_sa.at[i],
             recv_sem=sem_ra.at[w],
             device_id=(peer, b),
             device_id_type=MESH,
         )
 
-    def start_a(i, carry):
-        copy_a(along_walk(i)).start()
-        return carry
-
-    lax.fori_loop(0, ND - 1, start_a, 0)
-    recv_a[pl.ds(pl.multiple_of(w * NF, NF), NF), :] = send_a[w]
+    for i in range(ND - 1):
+        copy_a(i).start()
+    recv_a[pl.ds(pl.multiple_of(w * NF, NF), NF), :] = send_a[ND - 1]
+
+    def rotate(m, carry):
+        turn = ((m >> 2) * (sites[...] >> 2) + (m & 3) * (sites[...] & 3)) & 3
+        sign = (1 - (turn & 2)).astype(F32)
+        odd = (turn & 1).astype(F32)
+        along = jnp.broadcast_to((1.0 - odd) * sign, (NF, NV)).astype(BF16)
+        across = jnp.broadcast_to(odd * sign, (NF, NV)).astype(BF16)
+        cosine = base[0:NF]
+        sine = base[NF:PACK]
+        table[m, 0:NF, :] = cosine * along + sine * across
+        table[m, NF:PACK, :] = sine * along - cosine * across
+        return carry
+
+    lax.fori_loop(0, NM, rotate, 0)
 
     for part, target in ((0, outer_re), (1, outer_im)):
         for tile in range(NV // 128):
@@ -222,21 +240,12 @@
 
     mine = shift[w]
     for i in range(ND):
-        chosen[i] = shift[shift[lax.rem(along_blk(i) - w + ND, ND)]]
-
-    def arrive_a(i, carry):
-        peer = lax.rem(w + i, ND)
-        pltpu.make_async_remote_copy(
-            src_ref=send_a.at[peer],
-            dst_ref=recv_a.at[pl.ds(pl.multiple_of(peer * NF, NF), NF)],
-            send_sem=sem_sa.at[peer],
-            recv_sem=sem_ra.at[peer],
-            device_id=(peer, b),
-            device_id_type=MESH,
-        ).wait()
-        return carry
-
-    lax.fori_loop(1, ND, arrive_a, 0)
+        chosen[i] = shift[shift[(along_blk(i) - w) & (ND - 1)]]
+
+    for i in range(ND - 1):
+        peer = along_walk(i)
+        pltpu.make_async_copy(send_a.at[i], rows_from(peer), sem_ra.at[peer]).wait()
+        copy_a(i).wait_send()
 
     def copy_d(m):
         return pltpu.make_async_remote_copy(
@@ -244,7 +253,7 @@
             dst_ref=recv_d.at[b],
             send_sem=sem_sd.at[m],
             recv_sem=sem_rd.at[b],
-            device_id=(m, lax.rem(w + m, ND)),
+            device_id=(m, (w + m) & (ND - 1)),
             device_id_type=MESH,
         )
 
@@ -256,48 +265,48 @@
 
     diagonal = jnp.where(jnp.logical_and(left, row_of == lane_of), 1.0, 0.0)
 
-    def assemble(group, carry):
-        momenta = [4 * group + k for k in range(4)]
-        rows = jnp.concatenate([table[m] for m in momenta], axis=0)
-        raw = jnp.dot(rows, recv_a[...], preferred_element_type=F32)
-        for k, m in enumerate(momenta):
-            part = raw[k * PACK : k * PACK + NF] + swap(raw[k * PACK + NF : (k + 1) * PACK]) * minus_left
+    def assemble(group):
+        raw = held.at[group % 2]
+        for k in range(4):
+            m = 4 * group + k
+            part = raw[k * PACK : k * PACK + NF, :] + swap(raw[k * PACK + NF : (k + 1) * PACK, :]) * minus_left
             part = part + diagonal * (mine == m).astype(F32)
-            start = pl.multiple_of(m * NF, NF)
-            value = outer_re[pl.ds(start, NF), :] * part + outer_im[pl.ds(start, NF), :] * swap(part)
+            rows = slice(m * NF, m * NF + NF)
+            value = outer_re[rows, :] * part + outer_im[rows, :] * swap(part)
             green[m] = value.astype(BF16)
             send_d[m] = pick(value, skew).astype(BF16)
-        for m in momenta:
-
-            @pl.when(jnp.logical_not(is_own(m)))
-            def _():
-                copy_d(m).start()
-
-            @pl.when(is_own(m))
-            def _():
-                own_d(m).start()
-
-        return carry
-
-    lax.fori_loop(0, NM // 4, assemble, 0)
-
-    def copy_t(peer):
+
+    for group in range(NM // 4 + 1):
+        if group < NM // 4:
+            held[group % 2] = jnp.dot(
+                table[4 * group : 4 * group + 4].reshape(4 * PACK, NV), recv_a[...], preferred_element_type=F32
+            )
+        if group > 0:
+            assemble(group - 1)
+            for k in range(4):
+                m = 4 * (group - 1) + k
+
+                @pl.when(jnp.logical_not(is_own(m)))
+                def _():
+                    copy_d(m).start()
+
+    @pl.when(alone)
+    def _():
+        own_d(w).start()
+
+    def copy_t(i):
         return pltpu.make_async_remote_copy(
-            src_ref=send_t.at[peer],
+            src_ref=send_t.at[i],
             dst_ref=recv_t.at[b],
-            send_sem=sem_st.at[peer],
+            send_sem=sem_st.at[i],
             recv_sem=sem_rt.at[b],
-            device_id=(w, peer),
+            device_id=(w, along_blk(i)),
             device_id_type=MESH,
         )
 
-    def start_t(i, carry):
-        peer = along_blk(i)
-        send_t[peer] = green[chosen[i]]
-        copy_t(peer).start()
-        return carry
-
-    lax.fori_loop(0, ND - 1, start_t, 0)
+    for i in range(ND - 1):
+        send_t[i] = green[chosen[i]]
+        copy_t(i).start()
     recv_t[b] = green[chosen[ND - 1]]
 
     def arrive_b(u, carry):
@@ -323,18 +332,24 @@
 
     lax.fori_loop(0, NM // 2, pair_up, 0)
 
-    def copy_o(peer):
+    def peer_o(i):
+        step = i >> 2
+        y = (b >> 1) + 2 - step + 3 * (step >> 1) - 2 * (step & (step >> 1))
+        x = (b >> 3) + 1 - ((i & 3) >> 1)
+        return ((x & 1) << 3) + ((y & 3) << 1) + ((b + i + 1) & 1)
+
+    def copy_o(i):
         return pltpu.make_async_remote_copy(
-            src_ref=send_o.at[peer],
+            src_ref=send_o.at[i],
             dst_ref=out.at[source],
-            send_sem=sem_so.at[peer],
+            send_sem=sem_so.at[i],
             recv_sem=sem_ro.at[source],
-            device_id=(w, peer),
+            device_id=(w, peer_o(i)),
             device_id_type=MESH,
         )
 
     def window(i, carry):
-        peer = along_blk(i)
+        peer = peer_o(i)
         offsets = [transfers[2 * peer + k] for k in range(2)]
 
         def multiply(step, carry):
@@ -364,16 +379,16 @@
             col = lane_of + nu
             keep = (row >= 0) & (row < NF) & (col >= 0) & (col < NF)
             result = pick(jnp.where(left, sum_re, sum_im), straight)
-            send_o[peer, k] = jnp.where(keep, result, 0.0).astype(BF16)
+            send_o[i, k] = jnp.where(keep, result, 0.0).astype(BF16)
 
         @pl.when(i < ND - 1)
         def _():
-            copy_o(peer).start()
+            copy_o(i).start()
 
         return carry
 
     lax.fori_loop(0, ND, window, 0)
-    own_o = pltpu.make_async_copy(send_o.at[b], out.at[source], sem_ro.at[source])
+    own_o = pltpu.make_async_copy(send_o.at[ND - 1], out.at[source], sem_ro.at[source])
     own_o.start()
 
     def arrive_o(i, carry):
@@ -382,13 +397,9 @@
 
     lax.fori_loop(0, ND, arrive_o, 0)
 
-    def drain(i, carry):
-        peer = lax.rem(b + i, ND)
-        copy_t(peer).wait_send()
-        copy_o(peer).wait_send()
-        return carry
-
-    lax.fori_loop(1, ND, drain, 0)
+    for i in range(ND - 1):
+        copy_t(i).wait_send()
+        copy_o(i).wait_send()
 
     def drain_d(m, carry):
         @pl.when(jnp.logical_not(is_own(m)))
@@ -433,14 +444,17 @@
             pltpu.VMEM((2, NV), F32),
             pltpu.SMEM((NM,), jnp.int32),
             pltpu.SMEM((NQ,), jnp.int32),
-            pltpu.VMEM((2, NF, NV), BF16),
+            pltpu.VMEM((2, 16, NV), F32),
+            pltpu.VMEM((PACK, NV), BF16),
+            pltpu.VMEM((NM, NF, PACK), F32),
+            blocks,
             pltpu.VMEM((NM, PACK, NV), BF16),
             pltpu.VMEM((NV, PACK), F32),
             pltpu.VMEM((NV, PACK), F32),
-            pltpu.VMEM((NM, 8, PACK), F32),
             pltpu.SMEM((NM,), jnp.int32),
             blocks,
             pltpu.VMEM((NV, PACK), BF16),
+            pltpu.VMEM((2, 4 * PACK, PACK), F32),
             blocks,
             blocks,
             blocks,

time: 46.3 us -> 43 us (0.929)
  Pallas kernels: 46.2 us -> 42.8 us
    pallas_call x1, Pallas kernels: 43.9 us -> 40.6 us  [shards(): pl.pallas_call(kernel, out_shape=[jax.ShapeDtypeStruct((ND, 2, NF, PACK),...]
where the time goes in v4:
time: 43 us; the launch traced here: 42.8 us
  Pallas kernels  42.8 us (100%)
    pallas_call x1, Pallas kernels, shards(): pl.pallas_call(kernel, out_shape=[jax.ShapeDtypeStruct((ND, 2, NF, PACK),...  40.6 us
    pallas_call x1, Pallas kernels, shards(): pl.pallas_call(spread_out, out_shape=jax.ShapeDtypeStruct((2, 2, NF, NV),...  2.26 us

profile of v4, /device:TPU:1, one launch (start us, length us, event | category | flops | bytes accessed | tf_op | source)
XLA Modules:
  0.0 42.8 jit_solution(6091365111523115910)
XLA Ops:
  0.0 40.6 %shard_map.64 = (bf16[16,2,64,128]{3,2,1,0:T(8,128)(2,1)}, s32[16]{0:T(128)}) custom-call(s32[1,1024]{1,0:T(1,128)} %times_in.1, s32[1,1024]{1,0:T(1,128)} %sites_in.1, bf16[1,64,1024]{2,1,0:T(8,128)(2,1)} %matrix_in.1, f32[2,1024]{1,0:T(2,128)} %bare_in.1, s32[16]{0:T(128)} %shift_in.1, s32[32]{0:T(128)} %transfers_in.1), custom_call_target="tpu_custom_call" | custom-call | tf_op jit(solution)/shard_map/pallas_call | solution.py:432
  40.6 2.3 %shard_map.65 = f32[2,2,64,1024]{3,2,1,0:T(8,128)} custom-call(s32[16]{0:T(128)} %get-tuple-element.7.inverse, bf16[16,2,64,128]{3,2,1,0:T(8,128)(2,1)} %get-tuple-element.8.blocks), custom_call_target="tpu_custom_call" | custom-call | tf_op jit(solution)/shard_map/pallas_call | solution.py:474

commit v5 on v4

--- a/solution.py
+++ b/solution.py
@@ -64,6 +64,7 @@
     factor,
     base,
     partial,
+    column,
     projected,
     table,
     outer_re,
@@ -163,6 +164,12 @@
         apart, turned = blocks[0] - blocks[2], quarter(blocks[1] - blocks[3])
         return even + odd, apart + turned, even - odd, apart - turned
 
+    for m in range(NM):
+        piece_re = bare[0:1, m * NF : m * NF + NF] * scale
+        piece_im = bare[1:2, m * NF : m * NF + NF] * scale
+        column[m, 0:1, :] = jnp.concatenate([piece_re, -piece_re], axis=1)
+        column[m, 1:2, :] = jnp.concatenate([piece_im, piece_im], axis=1)
+
     for x in range(SIDE):
         rows = []
         for y in range(SIDE):
@@ -173,15 +180,13 @@
         )
         for y, value in enumerate(turns([block[NF * y : NF * y + NF] for y in range(SIDE)])):
             partial[SIDE * x + y] = value
-    for y in range(SIDE):
+    def join(y, carry):
         for x, value in enumerate(turns([partial[SIDE * x + y] for x in range(SIDE)])):
-            m = SIDE * x + y
-            piece_re = bare[0:1, m * NF : m * NF + NF] * scale
-            piece_im = bare[1:2, m * NF : m * NF + NF] * scale
-            value = value * jnp.concatenate([piece_re, -piece_re], axis=1) + swap(value) * jnp.concatenate(
-                [piece_im, piece_im], axis=1
-            )
-            projected[m] = value.astype(BF16)
+            factors = column[SIDE * x + y]
+            projected[SIDE * x + y] = (value * factors[0:1] + swap(value) * factors[1:2]).astype(BF16)
+        return carry
+
+    lax.fori_loop(0, SIDE, join, 0)
     for i in range(ND):
         send_a[i] = projected[shift[along_walk(i)]]
 
@@ -318,19 +323,21 @@
 
         return carry
 
-    def pair_up(pair, carry):
-        arrive_b(2 * pair, 0)
-        arrive_b(2 * pair + 1, 0)
-        even = recv_d[2 * pair].astype(F32)
-        other = recv_d[2 * pair + 1].astype(F32)
-        direct_re[pair] = jnp.where(left, even, swap(other))
-        direct_im[pair] = jnp.where(left, swap(even), other)
-        both = recv_t[pl.ds(2 * pair, 2)].astype(F32).reshape(2 * NF, PACK).T
-        turned_re[pair, 16 : 16 + NF, :] = pick(both[0:NF], skew)
-        turned_im[pair, 16 : 16 + NF, :] = pick(both[NF:PACK], skew)
-        return carry
-
-    lax.fori_loop(0, NM // 2, pair_up, 0)
+    def pair_up(step, carry):
+        for u in range(16):
+            arrive_b(16 * step + u, 0)
+        for k in range(8):
+            pair = 8 * step + k
+            even = recv_d[2 * pair].astype(F32)
+            other = recv_d[2 * pair + 1].astype(F32)
+            direct_re[pair] = jnp.where(left, even, swap(other))
+            direct_im[pair] = jnp.where(left, swap(even), other)
+            both = recv_t[pl.ds(2 * pair, 2)].astype(F32).reshape(2 * NF, PACK).T
+            turned_re[pair, 16 : 16 + NF, :] = pick(both[0:NF], skew)
+            turned_im[pair, 16 : 16 + NF, :] = pick(both[NF:PACK], skew)
+        return carry
+
+    lax.fori_loop(0, NM // 16, pair_up, 0)
 
     def peer_o(i):
         step = i >> 2
@@ -435,7 +442,7 @@
             jax.ShapeDtypeStruct((ND, 2, NF, PACK), BF16),
             jax.ShapeDtypeStruct((NM,), jnp.int32),
         ],
-        in_specs=[here] * 6,
+        in_specs=[pl.BlockSpec(memory_space=pltpu.HBM)] * 6,
         out_specs=[here, smem],
         scratch_shapes=[
             pltpu.VMEM((1, NV), jnp.int32),
@@ -447,6 +454,7 @@
             pltpu.VMEM((2, 16, NV), F32),
             pltpu.VMEM((PACK, NV), BF16),
             pltpu.VMEM((NM, NF, PACK), F32),
+            pltpu.VMEM((NM, 8, PACK), F32),
             blocks,
             pltpu.VMEM((NM, PACK, NV), BF16),
             pltpu.VMEM((NV, PACK), F32),
@@ -469,13 +477,14 @@
             pltpu.SemaphoreType.DMA((6,)),
         ]
         + [sems] * 8,
-        compiler_params=pltpu.CompilerParams(collective_id=0, has_side_effects=True),
-    )(vertex_times, vertex_sites, vertex_matrix, bare_green, transfer_momentum, transfers)
+        compiler_params=pltpu.CompilerParams(collective_id=0, has_side_effects=True, vmem_limit_bytes=24 * 2**20),
+    )(*[pltpu.with_memory_space_constraint(a, pltpu.HBM) for a in (vertex_times, vertex_sites, vertex_matrix, bare_green, transfer_momentum, transfers)])
     return pl.pallas_call(
         spread_out,
         out_shape=jax.ShapeDtypeStruct((2, 2, NF, NV), F32),
         in_specs=[smem, vmem],
         out_specs=vmem,
+        compiler_params=pltpu.CompilerParams(vmem_limit_bytes=16 * 2**20),
     )(inverse, results)
 
 

time: 43 us -> 41.6 us (0.967)
  Pallas kernels: 42.8 us -> 41.6 us
    pallas_call x1, Pallas kernels: 40.6 us -> 39.8 us  [shards(): pl.pallas_call(kernel, out_shape=[jax.ShapeDtypeStruct((ND, 2, NF, PACK),...]
    pallas_call x1, Pallas kernels: 2.26 us -> 1.75 us  [shards(): pl.pallas_call(spread_out, out_shape=jax.ShapeDtypeStruct((2, 2, NF, NV),...]
where the time goes in v5:
time: 41.6 us
  Pallas kernels  41.6 us (100%)
    pallas_call x1, Pallas kernels, shards(): pl.pallas_call(kernel, out_shape=[jax.ShapeDtypeStruct((ND, 2, NF, PACK),...  39.8 us
    pallas_call x1, Pallas kernels, shards(): pl.pallas_call(spread_out, out_shape=jax.ShapeDtypeStruct((2, 2, NF, NV),...  1.75 us

profile of v5, /device:TPU:1, one launch (start us, length us, event | category | flops | bytes accessed | tf_op | source)
XLA Modules:
  0.0 41.6 jit_solution(3250406702600070048)
XLA Ops:
  0.0 39.8 %shard_map.64 = (bf16[16,2,64,128]{3,2,1,0:T(8,128)(2,1)S(1)}, s32[16]{0:T(128)S(1)}) custom-call(s32[1,1024]{1,0:T(1,128)} %times_in.1, s32[1,1024]{1,0:T(1,128)} %sites_in.1, bf16[1,64,1024]{2,1,0:T(8,128)(2,1)} %matrix_in.1, f32[2,1024]{1,0:T(2,128)} %bare_in.1, s32[16]{0:T(128)} %shift_in.1, s32[32]{0:T(128)} %transfers_in.1), custom_call_target="tpu_custom_call" | custom-call | tf_op jit(solution)/shard_map/pallas_call | solution.py:439
  39.8 1.7 %shard_map.65 = f32[2,2,64,1024]{3,2,1,0:T(8,128)} custom-call(s32[16]{0:T(128)S(1)} %get-tuple-element.7.inverse, bf16[16,2,64,128]{3,2,1,0:T(8,128)(2,1)S(1)} %get-tuple-element.8.blocks), custom_call_target="tpu_custom_call" | custom-call | tf_op jit(solution)/shard_map/pallas_call | solution.py:482

commit v6 on v5

--- a/solution.py
+++ b/solution.py
@@ -218,8 +218,8 @@
         across = jnp.broadcast_to(odd * sign, (NF, NV)).astype(BF16)
         cosine = base[0:NF]
         sine = base[NF:PACK]
-        table[m, 0:NF, :] = cosine * along + sine * across
-        table[m, NF:PACK, :] = sine * along - cosine * across
+        table[m, :, 0:NV] = cosine * along + sine * across
+        table[m, :, NV : 2 * NV] = sine * along - cosine * across
         return carry
 
     lax.fori_loop(0, NM, rotate, 0)
@@ -251,6 +251,9 @@
         peer = along_walk(i)
         pltpu.make_async_copy(send_a.at[i], rows_from(peer), sem_ra.at[peer]).wait()
         copy_a(i).wait_send()
+    whole = recv_a[0:NV, :].astype(F32)
+    sign = jnp.where(lax.broadcasted_iota(jnp.int32, (1, PACK), 1) < NF, -1.0, 1.0)
+    recv_a[NV : 2 * NV, :] = (swap(whole) * sign).astype(BF16)
 
     def copy_d(m):
         return pltpu.make_async_remote_copy(
@@ -274,8 +277,7 @@
         raw = held.at[group % 2]
         for k in range(4):
             m = 4 * group + k
-            part = raw[k * PACK : k * PACK + NF, :] + swap(raw[k * PACK + NF : (k + 1) * PACK, :]) * minus_left
-            part = part + diagonal * (mine == m).astype(F32)
+            part = raw[k * NF : (k + 1) * NF, :] + diagonal * (mine == m).astype(F32)
             rows = slice(m * NF, m * NF + NF)
             value = outer_re[rows, :] * part + outer_im[rows, :] * swap(part)
             green[m] = value.astype(BF16)
@@ -284,7 +286,7 @@
     for group in range(NM // 4 + 1):
         if group < NM // 4:
             held[group % 2] = jnp.dot(
-                table[4 * group : 4 * group + 4].reshape(4 * PACK, NV), recv_a[...], preferred_element_type=F32
+                table[4 * group : 4 * group + 4].reshape(4 * NF, 2 * NV), recv_a[...], preferred_element_type=F32
             )
         if group > 0:
             assemble(group - 1)
@@ -456,13 +458,13 @@
             pltpu.VMEM((NM, NF, PACK), F32),
             pltpu.VMEM((NM, 8, PACK), F32),
             blocks,
-            pltpu.VMEM((NM, PACK, NV), BF16),
+            pltpu.VMEM((NM, NF, 2 * NV), BF16),
             pltpu.VMEM((NV, PACK), F32),
             pltpu.VMEM((NV, PACK), F32),
             pltpu.SMEM((NM,), jnp.int32),
             blocks,
-            pltpu.VMEM((NV, PACK), BF16),
-            pltpu.VMEM((2, 4 * PACK, PACK), F32),
+            pltpu.VMEM((2 * NV, PACK), BF16),
+            pltpu.VMEM((2, 4 * NF, PACK), F32),
             blocks,
             blocks,
             blocks,

time: 41.6 us -> 41.1 us (0.988)
  Pallas kernels: 41.6 us -> 41 us
    pallas_call x1, Pallas kernels: 39.8 us -> 39.3 us  [shards(): pl.pallas_call(kernel, out_shape=[jax.ShapeDtypeStruct((ND, 2, NF, PACK),...]
where the time goes in v6:
time: 41.1 us; the launch traced here: 41 us
  Pallas kernels  41 us (100%)
    pallas_call x1, Pallas kernels, shards(): pl.pallas_call(kernel, out_shape=[jax.ShapeDtypeStruct((ND, 2, NF, PACK),...  39.3 us
    pallas_call x1, Pallas kernels, shards(): pl.pallas_call(spread_out, out_shape=jax.ShapeDtypeStruct((2, 2, NF, NV),...  1.75 us

profile of v6, /device:TPU:1, one launch (start us, length us, event | category | flops | bytes accessed | tf_op | source)
XLA Modules:
  0.0 41.0 jit_solution(15633321636169512103)
XLA Ops:
  0.0 39.3 %shard_map.64 = (bf16[16,2,64,128]{3,2,1,0:T(8,128)(2,1)S(1)}, s32[16]{0:T(128)S(1)}) custom-call(s32[1,1024]{1,0:T(1,128)} %times_in.1, s32[1,1024]{1,0:T(1,128)} %sites_in.1, bf16[1,64,1024]{2,1,0:T(8,128)(2,1)} %matrix_in.1, f32[2,1024]{1,0:T(2,128)} %bare_in.1, s32[16]{0:T(128)} %shift_in.1, s32[32]{0:T(128)} %transfers_in.1), custom_call_target="tpu_custom_call" | custom-call | tf_op jit(solution)/shard_map/pallas_call | solution.py:441
  39.3 1.7 %shard_map.65 = f32[2,2,64,1024]{3,2,1,0:T(8,128)} custom-call(s32[16]{0:T(128)S(1)} %get-tuple-element.7.inverse, bf16[16,2,64,128]{3,2,1,0:T(8,128)(2,1)S(1)} %get-tuple-element.8.blocks), custom_call_target="tpu_custom_call" | custom-call | tf_op jit(solution)/shard_map/pallas_call | solution.py:484

commit v7 on v6

--- a/solution.py
+++ b/solution.py
@@ -342,10 +342,11 @@
     lax.fori_loop(0, NM // 16, pair_up, 0)
 
     def peer_o(i):
-        step = i >> 2
-        y = (b >> 1) + 2 - step + 3 * (step >> 1) - 2 * (step & (step >> 1))
-        x = (b >> 3) + 1 - ((i & 3) >> 1)
-        return ((x & 1) << 3) + ((y & 3) << 1) + ((b + i + 1) & 1)
+        up = jnp.where(i < 4, 2, jnp.where(i < 12, 1 + 2 * (i & 1), 0))
+        q = jnp.where(jnp.logical_and(i >= 4, i < 12), (i - 4) >> 1, i & 3)
+        y = (b >> 1) + up
+        x = (b >> 3) + 1 - (q >> 1)
+        return ((x & 1) << 3) + ((y & 3) << 1) + ((b + q + 1) & 1)
 
     def copy_o(i):
         return pltpu.make_async_remote_copy(

time: 41.1 us -> 41.1 us (level)
  no operation moved by 1% of the time
where the time goes in v7:
time: 41.1 us; the launch traced here: 41 us
  Pallas kernels  41 us (100%)
    pallas_call x1, Pallas kernels, shards(): pl.pallas_call(kernel, out_shape=[jax.ShapeDtypeStruct((ND, 2, NF, PACK),...  39.2 us
    pallas_call x1, Pallas kernels, shards(): pl.pallas_call(spread_out, out_shape=jax.ShapeDtypeStruct((2, 2, NF, NV),...  1.75 us

profile of v7, /device:TPU:1, one launch (start us, length us, event | category | flops | bytes accessed | tf_op | source)
XLA Modules:
  0.0 41.0 jit_solution(2431983092758808352)
XLA Ops:
  0.0 39.2 %shard_map.64 = (bf16[16,2,64,128]{3,2,1,0:T(8,128)(2,1)S(1)}, s32[16]{0:T(128)S(1)}) custom-call(s32[1,1024]{1,0:T(1,128)} %times_in.1, s32[1,1024]{1,0:T(1,128)} %sites_in.1, bf16[1,64,1024]{2,1,0:T(8,128)(2,1)} %matrix_in.1, f32[2,1024]{1,0:T(2,128)} %bare_in.1, s32[16]{0:T(128)} %shift_in.1, s32[32]{0:T(128)} %transfers_in.1), custom_call_target="tpu_custom_call" | custom-call | tf_op jit(solution)/shard_map/pallas_call | solution.py:442
  39.3 1.7 %shard_map.65 = f32[2,2,64,1024]{3,2,1,0:T(8,128)} custom-call(s32[16]{0:T(128)S(1)} %get-tuple-element.7.inverse, bf16[16,2,64,128]{3,2,1,0:T(8,128)(2,1)S(1)} %get-tuple-element.8.blocks), custom_call_target="tpu_custom_call" | custom-call | tf_op jit(solution)/shard_map/pallas_call | solution.py:485
